TPU v7x, 32 devices: a whole 2x2x4 slice. The times are simulated.
32 devices in a mesh: row: 8 (over z, core), col: 4 (over y, x).
Axes of the slice: x: 2, y: 2, z: 4, core: 2. Of those that a mesh axis runs over, the one named last changes fastest.
Arguments:
- points: bfloat16 [2048, 1024], P(('row', 'col')), may hold values from -6 to 6
- factor: float32 [2048, 256], P(('row', 'col')), may hold values from 0 to 1
Outputs:
- factor_out: float32 [2048, 256], P(('row', 'col'))
All inputs are finite; a program needn't handle non-finite values.
Results may differ from a plain program's by a relative error of at most 0.002.
The roundings to bfloat16 on the way count: a program that leaves them out, or rounds other values in their place, can miss the bound.
Values may be sent and summed in bfloat16 or wider, within the bound.
A program may use at most 64 MiB of HBM per device.

v0:
```python
import math
import jax
import jax.numpy as jnp
from jax import lax
from jax.sharding import PartitionSpec as P

EMBED_WIDTH = 1024
ITERS = 2


def shards(points, factor):
    nrow = lax.axis_size("row")
    ncol = lax.axis_size("col")
    pts = points.shape[0]
    rank = factor.shape[1]
    total = pts * nrow * ncol
    row_pts = lax.all_gather(points, "col", axis=0, tiled=True)
    col_pts = lax.all_gather(points, "row", axis=0, tiled=True)
    gram_matrix = lax.dot_general(
        row_pts, col_pts, (((1,), (1,)), ((), ())), preferred_element_type=jnp.float32
    )
    row_sq = jnp.sum(jnp.square(row_pts.astype(jnp.float32)), axis=1)
    col_sq = jnp.sum(jnp.square(col_pts.astype(jnp.float32)), axis=1)
    kern = jnp.exp((2.0 * gram_matrix - row_sq[:, None] - col_sq[None, :]) * (0.5 / EMBED_WIDTH))
    row_sum, band = lax.psum((jnp.sum(kern, axis=1), jnp.sum(kern)), "col")
    col_sum, grand = lax.psum((jnp.sum(kern, axis=0), band), "row")
    affinity = (
        kern - row_sum[:, None] / total - col_sum[None, :] / total + grand / (total * total)
    ).astype(jnp.bfloat16)
    unit = 2.0 / math.sqrt(total * rank)
    h = factor * unit
    for step in range(ITERS):
        hb = h.astype(jnp.bfloat16)
        copies = lax.all_gather(hb, "row", axis=0, tiled=True)
        ah = lax.psum_scatter(
            jnp.dot(affinity, copies, preferred_element_type=jnp.float32),
            "col",
            scatter_dimension=0,
            tiled=True,
        )
        local_gram = lax.dot_general(
            h, h, (((0,), (0,)), ((), ())), precision=lax.Precision.HIGHEST
        )
        hh = lax.psum(local_gram, ("row", "col"))
        scale = 0.5 / jnp.sqrt(jnp.sum(hh * hh) + 1e-06)
        h = jnp.maximum(h - scale * (jnp.dot(h, hh, precision=lax.Precision.HIGHEST) - ah), 0.0)
    return h / unit


def solution(mesh):
    in_specs = (P(("row", "col"), None), P(("row", "col"), None))
    out_specs = P(("row", "col"), None)
    return jax.shard_map(shards, mesh=mesh, in_specs=in_specs, out_specs=out_specs, check_vma=False)
```

profile of v0, /device:TPU:0, one launch (start us, length us, event | category | flops | bytes accessed | tf_op | source)
XLA Modules:
  0.0 301.0 jit_solution(7194826416192646812)
XLA Ops:
  7.4 0.0 copy-start.1
  7.4 0.0 all-gather.2.cloned.1.call-start
  7.4 0.7 all-gather.2.cloned.1.call-update
  8.1 0.0 all-reduce.5.cloned.1.call-start
  8.1 2.0 fusion.12
  10.2 0.0 all-reduce.5.cloned.1.call-update
  10.2 0.0 reduce-scatter.3.cloned.1.call-start
  10.3 11.9 %all_gather.12 = bf16[256,1024]{1,0:T(8,128)(2,1)S(1)} all-gather(bf16[64,1024]{1,0:T(8,128)(2,1)} %param.2), channel_id=1, replica_groups=mesh['row'=8,'col'=4] {'col'}, dimensions={0}, use_global_device_ids=true | all-gather | bytes 655360 | tf_op jit(solution)/shard_map/all_gather | solution.py:17
  22.1 0.0 copy-done.1
  22.2 0.2 multiply_reduce_fusion.1
  22.3 15.2 %all_gather.14 = bf16[512,256]{1,0:T(8,128)(2,1)S(1)} all-gather(bf16[64,256]{1,0:T(8,128)(2,1)S(1)} %multiply_convert_fusion), channel_id=1, replica_groups=mesh['row'=8,'col'=4] {'row'}, dimensions={0}, use_global_device_ids=true | all-gather | bytes 294912 | tf_op jit(solution)/shard_map/all_gather | solution.py:34
  37.6 0.0 all-gather.2.cloned.1.call-done
  37.6 0.0 copy-start
  37.6 1.6 multiply_reduce_fusion
  39.2 0.0 copy-done
  39.2 1.2 fusion.20
  40.4 9.6 %all-reduce.1 = (f32[]{:T(128)}, f32[256]{0:T(256)S(1)}) all-reduce(f32[]{:T(128)} %get-tuple-element.6, f32[256]{0:T(256)S(1)} %get-tuple-element.5), channel_id=1, replica_groups=mesh['row'=8,'col'=4] {'col'}, use_global_device_ids=true, to_apply=%region_9.0 | all-reduce | flops 257 | bytes 2056 | tf_op jit(solution)/shard_map/psum | solution.py:25
  50.0 15.4 %all-reduce = (f32[]{:T(128)}, f32[512]{0:T(512)S(1)}) all-reduce(f32[]{:T(128)} %get-tuple-element.10, f32[512]{0:T(512)S(1)} %get-tuple-element.7), channel_id=1, replica_groups=mesh['row'=8,'col'=4] {'row'}, use_global_device_ids=true, to_apply=%region_10.0 | all-reduce | flops 513 | bytes 4104 | tf_op jit(solution)/shard_map/psum | solution.py:26
  66.1 1.0 fusion.19
  67.1 0.0 reduce-scatter.3.cloned.1.call-update
  67.1 0.0 all-reduce.7.cloned.1.call-start
  67.2 78.5 %all-reduce.5.cloned.1.call-done = f32[256,256]{1,0:T(8,128)} async-done(((f32[256,256]{1,0:T(8,128)}), f32[256,256]{1,0:T(8,128)}) %all-reduce.5.cloned.1.call-update) | async-done | bytes 262160 | tf_op jit(solution)/shard_map/psum | solution.py:44
  145.6 1.6 multiply_reduce_fusion.3
  147.9 0.0 reduce-scatter.3.cloned.1.call-done
  148.0 1.2 fusion.21
  149.2 14.2 %all_gather.15 = bf16[512,256]{1,0:T(8,128)(2,1)S(1)} all-gather(bf16[64,256]{1,0:T(8,128)(2,1)S(1)} %get-tuple-element.13), channel_id=1, replica_groups=mesh['row'=8,'col'=4] {'row'}, dimensions={0}, use_global_device_ids=true | all-gather | bytes 294912 | tf_op jit(solution)/shard_map/all_gather | solution.py:34
  163.4 1.1 fusion.22
  164.5 0.0 all-reduce.7.cloned.1.call-update
  164.5 0.0 reduce-scatter.5.cloned.1.call-start
  164.6 1.0 fusion.18
  165.6 0.0 reduce-scatter.5.cloned.1.call-update
  165.6 124.1 %all-reduce.7.cloned.1.call-done = f32[256,256]{1,0:T(8,128)} async-done(((f32[256,256]{1,0:T(8,128)}), f32[256,256]{1,0:T(8,128)}) %all-reduce.7.cloned.1.call-update) | async-done | bytes 262160 | tf_op jit(solution)/shard_map/psum | solution.py:44
  289.7 1.6 multiply_reduce_fusion.2
  292.0 0.0 reduce-scatter.5.cloned.1.call-done
  292.0 1.8 fusion.7
  (3 shorter events, 0.0 us)
Async XLA Ops:
  7.4 14.8 %copy-start.1 = (f32[64,256]{1,0:T(8,128)S(1)}, f32[64,256]{1,0:T(8,128)}, u32[]{:S(2)}) copy-start(f32[64,256]{1,0:T(8,128)} %param.3) | copy-start | bytes 196612
  7.4 30.2 %all-gather.2.cloned.1.call-start = ((), (), s32[]{:S(2)}) async-start(), calls=%async_computation.3 | async-start | bytes 1179648 | tf_op jit(solution)/shard_map/all_gather | solution.py:18
  8.1 137.5 %all-reduce.5.cloned.1.call-start = ((), (), s32[]{:S(2)}) async-start(), calls=%async_computation.2 | async-start | bytes 524288 | tf_op jit(solution)/shard_map/psum | solution.py:44
  10.2 137.8 %reduce-scatter.3.cloned.1.call-start = ((), (), s32[]{:S(2)}) async-start(), calls=%async_computation.4 | async-start | bytes 327680 | tf_op jit(solution)/shard_map/reduce_scatter | solution.py:35
  37.6 1.6 copy-start
  67.1 222.6 %all-reduce.7.cloned.1.call-start = ((), (), s32[]{:S(2)}) async-start(), calls=%async_computation.5 | async-start | bytes 524288 | tf_op jit(solution)/shard_map/psum | solution.py:44
  164.5 127.5 %reduce-scatter.5.cloned.1.call-start = ((), (), s32[]{:S(2)}) async-start(), calls=%async_computation.6 | async-start | bytes 327680 | tf_op jit(solution)/shard_map/reduce_scatter | solution.py:35
Sparse Core Ops, SparseCore 0:
  9.8 26.2 all-gather.1
  67.2 21.1 reduce-scatter.2
  168.1 23.4 reduce-scatter.4
Sparse Core Ops, SparseCore 1:
  14.1 131.5 all-reduce.4
  164.6 125.0 all-reduce.6
where the time goes:
time: 301 us
  waiting for transfers between devices  203 us (67%)
  blocking collectives  66.4 us (22%)
  between operations  16.6 us (6%)
  matrix products  9.4 us (3%)
  other arithmetic  5.03 us (2%)
    psum x2, waiting for transfers between devices, shards(): hh = lax.psum(local_gram, ('row', 'col'))  203 us
    all_gather x2, blocking collectives, shards(): copies = lax.all_gather(hb, 'row', axis=0, tiled=True)  29.4 us
    psum x1, blocking collectives, shards(): col_sum, grand = lax.psum((jnp.sum(kern, axis=0), band), 'row')  15.4 us
    all_gather x1, blocking collectives, shards(): row_pts = lax.all_gather(points, 'col', axis=0, tiled=True)  11.9 us
    psum x1, blocking collectives, shards(): row_sum, band = lax.psum((jnp.sum(kern, axis=1), jnp.sum(kern)), 'col')  9.6 us
  transfers between devices with their start and end apart: 5, of which 2 were waited for; matrix products, arithmetic and copies ran while one was open for 3% of the time, Pallas kernels for 0%

commit v1 on v0

--- a/solution.py
+++ b/solution.py
@@ -41,7 +41,7 @@
         local_gram = lax.dot_general(
             h, h, (((0,), (0,)), ((), ())), precision=lax.Precision.HIGHEST
         )
-        hh = lax.psum(local_gram, ("row", "col"))
+        hh = jnp.sum(lax.all_gather(local_gram, ("row", "col")), axis=0)
         scale = 0.5 / jnp.sqrt(jnp.sum(hh * hh) + 1e-06)
         h = jnp.maximum(h - scale * (jnp.dot(h, hh, precision=lax.Precision.HIGHEST) - ah), 0.0)
     return h / unit

time: 301 us -> 254 us (0.84)
  waiting for transfers between devices: 203 us -> 150 us
  other arithmetic: 5.03 us -> 11.7 us
    psum x2 -> x0, waiting for transfers between devices: 203 us -> none  [shards(): hh = lax.psum(local_gram, ('row', 'col'))]
    all_gather x0 -> x2, waiting for transfers between devices: none -> 108 us  [shards(): hh = jnp.sum(lax.all_gather(local_gram, ('row', 'col')), axis=0)]
    reduce_scatter x2, waiting for transfers between devices: 0.04 us -> 40.8 us  [shards(): lax.psum_scatter(jnp.dot(affinity, copies, preferred_element_type=jnp.flo...]
    reduce_sum x0 -> x2, other arithmetic: none -> 7.86 us  [shards(): hh = jnp.sum(lax.all_gather(local_gram, ('row', 'col')), axis=0)]
  transfers between devices with their start and end apart: 5 -> 5, of which waited for: 2 -> 4; matrix products, arithmetic and copies ran while one was open for 3% -> 7% of each run, Pallas kernels for 0% -> 0%
where the time goes in v1:
time: 254 us
  waiting for transfers between devices  150 us (59%)
  blocking collectives  66.5 us (26%)
  between operations  15.2 us (6%)
  other arithmetic  11.7 us (5%)
  matrix products  10.4 us (4%)
    all_gather x2, waiting for transfers between devices, shards(): hh = jnp.sum(lax.all_gather(local_gram, ('row', 'col')), axis=0)  108 us
    reduce_scatter x2, waiting for transfers between devices, shards(): lax.psum_scatter(jnp.dot(affinity, copies, preferred_element_type=jnp.flo...  40.8 us
    all_gather x2, blocking collectives, shards(): copies = lax.all_gather(hb, 'row', axis=0, tiled=True)  29.6 us
    psum x1, blocking collectives, shards(): col_sum, grand = lax.psum((jnp.sum(kern, axis=0), band), 'row')  15.5 us
    all_gather x1, blocking collectives, shards(): row_pts = lax.all_gather(points, 'col', axis=0, tiled=True)  11.9 us
    psum x1, blocking collectives, shards(): row_sum, band = lax.psum((jnp.sum(kern, axis=1), jnp.sum(kern)), 'col')  9.65 us
    reduce_sum x2, other arithmetic, shards(): hh = jnp.sum(lax.all_gather(local_gram, ('row', 'col')), axis=0)  7.86 us
  transfers between devices with their start and end apart: 5, of which 4 were waited for; matrix products, arithmetic and copies ran while one was open for 7% of the time, Pallas kernels for 0%

profile of v1, /device:TPU:0, one launch (start us, length us, event | category | flops | bytes accessed | tf_op | source)
XLA Modules:
  0.0 253.8 jit_solution(12780438340869378497)
XLA Ops:
  6.5 0.0 copy-start
  6.5 0.0 all-gather.6.cloned.1.call-start
  6.5 0.7 all-gather.6.cloned.1.call-update
  7.3 0.0 all-gather.8.cloned.1.call-start
  7.3 2.0 fusion.12
  9.3 0.0 all-gather.8.cloned.1.call-update
  9.4 0.0 reduce-scatter.3.cloned.1.call-start
  9.4 11.9 %all_gather.26 = bf16[256,1024]{1,0:T(8,128)(2,1)S(1)} all-gather(bf16[64,1024]{1,0:T(8,128)(2,1)} %param.2), channel_id=1, replica_groups=mesh['row'=8,'col'=4] {'col'}, dimensions={0}, use_global_device_ids=true | all-gather | bytes 655360 | tf_op jit(solution)/shard_map/all_gather | solution.py:17
  21.3 0.8 multiply_convert_fusion
  22.1 15.2 %all_gather.28 = bf16[512,256]{1,0:T(8,128)(2,1)S(1)} all-gather(bf16[64,256]{1,0:T(8,128)(2,1)S(1)} %multiply_convert_fusion), channel_id=1, replica_groups=mesh['row'=8,'col'=4] {'row'}, dimensions={0}, use_global_device_ids=true | all-gather | bytes 294912 | tf_op jit(solution)/shard_map/all_gather | solution.py:34
  37.4 0.2 multiply_reduce_fusion.1
  37.5 0.0 all-gather.6.cloned.1.call-done
  37.6 1.5 multiply_reduce_fusion
  39.1 2.5 fusion.20
  41.5 9.6 %all-reduce.1 = (f32[]{:T(128)}, f32[256]{0:T(256)S(1)}) all-reduce(f32[]{:T(128)} %get-tuple-element.6, f32[256]{0:T(256)S(1)} %get-tuple-element.5), channel_id=1, replica_groups=mesh['row'=8,'col'=4] {'col'}, use_global_device_ids=true, to_apply=%region_9.0 | all-reduce | flops 257 | bytes 2056 | tf_op jit(solution)/shard_map/psum | solution.py:25
  51.2 15.5 %all-reduce = (f32[]{:T(128)}, f32[512]{0:T(512)S(1)}) all-reduce(f32[]{:T(128)} %get-tuple-element.10, f32[512]{0:T(512)S(1)} %get-tuple-element.7), channel_id=1, replica_groups=mesh['row'=8,'col'=4] {'row'}, use_global_device_ids=true, to_apply=%region_10.0 | all-reduce | flops 513 | bytes 4104 | tf_op jit(solution)/shard_map/psum | solution.py:26
  67.3 1.0 fusion.19
  68.3 0.0 reduce-scatter.3.cloned.1.call-update
  68.3 0.0 all-gather.10.cloned.1.call-start
  68.4 46.1 %all-gather.8.cloned.1.call-done = f32[8192,256]{1,0:T(8,128)} async-done(((f32[256,256]{1,0:T(8,128)}), f32[8192,256]{1,0:T(8,128)}) %all-gather.8.cloned.1.call-update) | async-done | bytes 8388624 | tf_op jit(solution)/shard_map/all_gather | solution.py:44
  114.5 3.9 %reduce_sum.81 = f32[256,256]{1,0:T(8,128)S(1)} reduce(f32[32,256,256]{2,1,0:T(8,128)} %bitcast.11, f32[]{:T(128)} %constant.4.clone.1), dimensions={0}, to_apply=%region_0.0 | reduce | flops 2031616 | bytes 8650756 | tf_op jit(solution)/shard_map/reduce_sum | solution.py:44
  118.4 0.7 multiply_reduce_fusion.3
  119.8 20.5 %reduce-scatter.3.cloned.1.call-done = f32[64,256]{1,0:T(8,128)} async-done(((f32[256,256]{1,0:T(8,128)}), f32[64,256]{1,0:T(8,128)}) %reduce-scatter.3.cloned.1.call-update) | async-done | bytes 65552 | tf_op jit(solution)/shard_map/reduce_scatter | solution.py:35
  140.3 0.0 copy-done
  140.3 1.1 fusion.21
  141.4 1.1 fusion.22
  142.5 0.0 all-gather.10.cloned.1.call-update
  142.5 0.0 reduce-scatter.5.cloned.1.call-start
  142.6 14.4 %all_gather.31 = bf16[512,256]{1,0:T(8,128)(2,1)S(1)} all-gather(bf16[64,256]{1,0:T(8,128)(2,1)S(1)} %get-tuple-element.13), channel_id=1, replica_groups=mesh['row'=8,'col'=4] {'row'}, dimensions={0}, use_global_device_ids=true | all-gather | bytes 294912 | tf_op jit(solution)/shard_map/all_gather | solution.py:34
  156.9 1.0 fusion.18
  157.9 0.0 reduce-scatter.5.cloned.1.call-update
  157.9 62.0 %all-gather.10.cloned.1.call-done = f32[8192,256]{1,0:T(8,128)} async-done(((f32[256,256]{1,0:T(8,128)}), f32[8192,256]{1,0:T(8,128)}) %all-gather.10.cloned.1.call-update) | async-done | bytes 8388624 | tf_op jit(solution)/shard_map/all_gather | solution.py:44
  220.0 3.9 %reduce_sum.88 = f32[256,256]{1,0:T(8,128)S(1)} reduce(f32[32,256,256]{2,1,0:T(8,128)} %bitcast.12, f32[]{:T(128)} %constant.4.clone.1), dimensions={0}, to_apply=%region_12.0 | reduce | flops 2031616 | bytes 8650756 | tf_op jit(solution)/shard_map/reduce_sum | solution.py:44
  223.9 0.7 multiply_reduce_fusion.2
  225.2 20.3 %reduce-scatter.5.cloned.1.call-done = f32[64,256]{1,0:T(8,128)} async-done(((f32[256,256]{1,0:T(8,128)}), f32[64,256]{1,0:T(8,128)}) %reduce-scatter.5.cloned.1.call-update) | async-done | bytes 65552 | tf_op jit(solution)/shard_map/reduce_scatter | solution.py:35
  245.6 1.7 fusion.7
  (2 shorter events, 0.0 us)
Async XLA Ops:
  6.5 133.7 %copy-start = (f32[64,256]{1,0:T(8,128)S(1)}, f32[64,256]{1,0:T(8,128)}, u32[]{:S(2)}) copy-start(f32[64,256]{1,0:T(8,128)} %param.3) | copy-start | bytes 196612
  6.5 31.0 %all-gather.6.cloned.1.call-start = ((), (), s32[]{:S(2)}) async-start(), calls=%async_computation.2 | async-start | bytes 1179648 | tf_op jit(solution)/shard_map/all_gather | solution.py:18
  7.3 107.3 %all-gather.8.cloned.1.call-start = ((), (), s32[]{:S(2)}) async-start(), calls=%async_computation.5 | async-start | bytes 8650752 | tf_op jit(solution)/shard_map/all_gather | solution.py:44
  9.4 130.9 %reduce-scatter.3.cloned.1.call-start = ((), (), s32[]{:S(2)}) async-start(), calls=%async_computation.3 | async-start | bytes 327680 | tf_op jit(solution)/shard_map/reduce_scatter | solution.py:35
  68.3 151.6 %all-gather.10.cloned.1.call-start = ((), (), s32[]{:S(2)}) async-start(), calls=%async_computation.6 | async-start | bytes 8650752 | tf_op jit(solution)/shard_map/all_gather | solution.py:44
  142.5 103.0 %reduce-scatter.5.cloned.1.call-start = ((), (), s32[]{:S(2)}) async-start(), calls=%async_computation.4 | async-start | bytes 327680 | tf_op jit(solution)/shard_map/reduce_scatter | solution.py:35
Sparse Core Ops, SparseCore 0:
  8.9 26.0 all-gather.5
  37.9 76.6 all-gather.7
  117.3 22.9 reduce-scatter.2
  143.0 76.9 all-gather.9
  222.6 22.9 reduce-scatter.4
